TPU v7x, 512 devices: a whole 4x4x16 slice. The times are simulated.
512 devices in a mesh: role: 4 (over y), pairs: 128 (over x, z, core).
Axes of the slice: x: 4, y: 4, z: 16, core: 2. Of those that a mesh axis runs over, the one named last changes fastest.
Arguments:
- three_index: bfloat16 [256, 1024, 512], P('pairs'), may hold values from -6 to 6
- coeff: bfloat16 [512, 512, 256], P('pairs'), may hold values from -6 to 6
- amps: bfloat16 [512, 256, 256], P('pairs'), may hold values from -4 to 4
- eps_virt: float32 [512, 256], P('pairs'), may hold values from 0.3 to 3
- eps_occ: float32 [256], replicated, may hold values from -1.5 to -0.3
- nvirt: int32 [512], P('pairs'), may hold values from 64 to 256, as said below
- pair_occ: int32 [512, 2], P('pairs'), may hold values from 0 to 255, as said below
- partners: int32 [512, 8], P('pairs'), may hold values from 0 to 511, as said below
- coupling: float32 [512, 8], P('pairs'), may hold values from -1 to 1
- pair_owner: int32 [512], P('pairs'), may hold values from 1 to 3, as said below
Outputs:
- amps_out: bfloat16 [1024, 256, 256], P(('role', 'pairs'))
- dressed_out: bfloat16 [1024, 512, 256], P(('role', 'pairs'))
Inputs may be any that keep to these rules, and one draw needn't show every extreme that they name: `nvirt`: each block of 4 consecutive pairs has one pair with all 256 virtuals. `pair_occ`: for pair k in block c = k // 4, the first orbital is one of the 2 orbitals numbered from 2 * c, and the second is one of the 6 orbitals numbered cyclically from 2 * (c - 1) modulo 256. Pair k's partners are distinct pairs of its own block of 4 pairs and the blocks just before and after it, cyclically modulo 512. `pair_owner`: in each block of 4 consecutive pairs, each of the roles 1 to 3 holds one or two pairs and exactly one role holds two.
All inputs are finite; a program needn't handle non-finite values.
Results may differ from a plain program's by a relative error of at most 0.012.
Values may be sent and summed in bfloat16 or wider, within the bound.
A program may use at most 64 MiB of HBM per device.

v0:
```python
import math
import jax
import jax.numpy as jnp
from jax import lax
from jax.sharding import PartitionSpec as P

PARTNERS = 8
ITERS = 2
SLOTS = 2


def extended(cells, sides, width):
    for axis, dim in sides:
        count = lax.axis_size(axis)
        head = lax.slice_in_dim(cells, 0, width, axis=dim)
        tail = lax.slice_in_dim(cells, cells.shape[dim] - width, cells.shape[dim], axis=dim)
        cells = jnp.concatenate(
            [
                lax.ppermute(tail, axis, [(i, (i + 1) % count) for i in range(count)]),
                cells,
                lax.ppermute(head, axis, [((i + 1) % count, i) for i in range(count)]),
            ],
            axis=dim,
        )
    return cells


def from_root(value, axis, source):
    kept = jnp.where(lax.axis_index(axis) == source, value, 0).astype(value.dtype)
    return lax.psum(kept, axis)


def local(
    three_index, coeff, amps, eps_virt, eps_occ, nvirt, pair_occ, partners, coupling, pair_owner
):
    column_count = lax.axis_size("pairs")
    role_index = lax.axis_index("role")
    column = lax.axis_index("pairs")
    occ_block = three_index.shape[0]
    width_aux = three_index.shape[1]
    pair_block = coeff.shape[0]
    width_pao = coeff.shape[1]
    width_virt = coeff.shape[2]
    slot_count = SLOTS
    pao_scale = 1.0 / math.sqrt(width_pao)
    aux_scale = 1.0 / math.sqrt(width_aux)
    virt_scale = 1.0 / math.sqrt(width_virt)
    occ_local = jnp.mod(pair_occ - (column - 1) * occ_block, occ_block * column_count)
    partner_local = jnp.mod(partners - (column - 1) * pair_block, pair_block * column_count)
    positions = jnp.arange(pair_block, dtype=jnp.int32)
    same_owner = (pair_owner[:, None] == pair_owner[None, :]).astype(jnp.int32)
    earlier = (positions[None, :] < positions[:, None]).astype(jnp.int32)
    pair_ranks = jnp.sum(same_owner * earlier, axis=1)
    gathered_at = pair_owner * slot_count + pair_ranks
    owned_here = pair_owner == role_index
    slot_ids = jnp.arange(slot_count, dtype=jnp.int32)
    slot_hits = (owned_here[None, :] & (pair_ranks[None, :] == slot_ids[:, None])).astype(jnp.int32)
    slot_pair = jnp.sum(slot_hits * positions[None, :], axis=1)
    slot_valid = (jnp.sum(slot_hits, axis=1) > 0).astype(jnp.float32)
    virtuals = jnp.arange(width_virt, dtype=jnp.int32)
    blocks = extended(three_index, (("pairs", 0),), occ_block)

    def transform_rows(orbitals_all, first_ids, second_ids):

        def one_pair(packed):
            orbitals, first_at, second_at = packed
            first_half = (
                jnp.dot(blocks[first_at], orbitals, preferred_element_type=jnp.float32) * pao_scale
            ).astype(jnp.bfloat16)
            second_half = (
                jnp.dot(blocks[second_at], orbitals, preferred_element_type=jnp.float32) * pao_scale
            ).astype(jnp.bfloat16)
            return (
                jnp.einsum("qa,qb->ab", first_half, second_half, preferred_element_type=jnp.float32)
                * aux_scale
            )

        return lax.map(one_pair, (orbitals_all, first_ids, second_ids))

    def transform(orbitals_all):
        return transform_rows(orbitals_all, occ_local[:, 0], occ_local[:, 1])

    near_orbitals = extended(coeff, (("pairs", 0),), pair_block)

    def slot_intersections():

        def slot_one_slot(slot_at):
            pair_at = slot_pair[slot_at]
            partner_orb = near_orbitals[partner_local[pair_at]]
            return (
                jnp.einsum(
                    "mb,kmc->kbc", coeff[pair_at], partner_orb, preferred_element_type=jnp.float32
                )
                * (1.0 / width_pao)
            ).astype(jnp.bfloat16)

        return lax.map(slot_one_slot, slot_ids)

    intersections = lax.cond(
        role_index > 0,
        slot_intersections,
        lambda: jnp.zeros((slot_count, PARTNERS, width_virt, width_virt), jnp.bfloat16),
    )

    def refresh(slot_ints, amp_pairs, near_amps):

        def refresh_one_slot(slot_at):
            pair_at = slot_pair[slot_at]
            intersection = intersections[slot_at]
            partner_amp = near_amps[partner_local[pair_at]]
            middle = jnp.einsum(
                "kbc,kcd->kbd", intersection, partner_amp, preferred_element_type=jnp.float32
            ).astype(jnp.bfloat16)
            partner_terms = jnp.einsum(
                "kbd,ked->kbe", middle, intersection, preferred_element_type=jnp.float32
            )
            coupled = jnp.sum(coupling[pair_at][:, None, None] * partner_terms, axis=0)
            occ_shift = eps_occ[pair_occ[pair_at, 0]] + eps_occ[pair_occ[pair_at, 1]]
            energy = eps_virt[pair_at][:, None] + eps_virt[pair_at][None, :] - occ_shift
            own_amp = amp_pairs[pair_at].astype(jnp.float32)
            fresh_amp = own_amp - (
                slot_ints[slot_at].astype(jnp.float32) + energy * own_amp + coupled
            ) / (energy + 1.0)
            keep_rows = (virtuals < nvirt[pair_at]).astype(jnp.float32) * slot_valid[slot_at]
            fresh_amp = (fresh_amp * keep_rows[:, None] * keep_rows[None, :]).astype(jnp.bfloat16)
            dressed = (
                (
                    coeff[pair_at].astype(jnp.float32)
                    + jnp.dot(coeff[pair_at], fresh_amp, preferred_element_type=jnp.float32)
                    * virt_scale
                )
                * slot_valid[slot_at]
            ).astype(jnp.bfloat16)
            return (fresh_amp, dressed)

        return lax.map(refresh_one_slot, slot_ids)

    zero_amp = jnp.zeros((slot_count, width_virt, width_virt), jnp.bfloat16)
    zero_orb = jnp.zeros((slot_count, width_pao, width_virt), jnp.bfloat16)
    amp_pairs = amps
    orb_pairs = coeff
    slot_amps = zero_amp
    slot_orbs = jnp.take(coeff, slot_pair, axis=0)
    for iteration in range(ITERS):
        local_ints = lax.cond(
            role_index == 0,
            lambda: transform(orb_pairs).astype(jnp.bfloat16),
            lambda: jnp.zeros((pair_block, width_virt, width_virt), jnp.bfloat16),
        )
        pair_ints = from_root(local_ints, "role", 0)
        slot_ints = jnp.take(pair_ints, slot_pair, axis=0)
        near_amps = extended(amp_pairs, (("pairs", 0),), pair_block)
        slot_amps, slot_orbs = lax.cond(
            role_index > 0,
            lambda: refresh(slot_ints, amp_pairs, near_amps),
            lambda: (zero_amp, zero_orb),
        )
        if iteration + 1 < ITERS:
            every_amp, every_orb = (
                lax.all_gather(slot_amps, "role", axis=0, tiled=True),
                lax.all_gather(slot_orbs, "role", axis=0, tiled=True),
            )
            amp_pairs = jnp.take(every_amp, gathered_at, axis=0)
            orb_pairs = jnp.take(every_orb, gathered_at, axis=0)
    return (slot_amps, slot_orbs)


def solution(mesh):
    in_specs = (
        P("pairs", None, None),
        P("pairs", None, None),
        P("pairs", None, None),
        P("pairs", None),
        P(),
        P("pairs"),
        P("pairs", None),
        P("pairs", None),
        P("pairs", None),
        P("pairs"),
    )
    out_specs = (P(("role", "pairs"), None, None), P(("role", "pairs"), None, None))
    return jax.shard_map(local, mesh=mesh, in_specs=in_specs, out_specs=out_specs, check_vma=False)
```

profile of v0, /device:TPU:16, one launch (start us, length us, event | category | flops | bytes accessed | tf_op | source)
XLA Modules:
  0.0 408.3 jit_solution(528838157583865312)
XLA Ops:
  7.2 1.9 collective-permute-start
  9.1 13.0 %collective-permute-start.1 = (bf16[2,1024,512]{2,1,0:T(8,128)(2,1)}, bf16[2,1024,512]{2,1,0:T(8,128)(2,1)S(1)}, u32[]{:S(2)}, u32[]{:S(2)}) collective-permute-start(bf16[2,1024,512]{2,1,0:T(8,128)(2,1)} %param.32), channel_id=1, source_target_pairs={{1,0},{2,1},{3,2},{4,3},{5,4},{6,5},{7,6},{8,7},{9,8},{10,9},{11,1... | collective-permute-start | bytes 6291464 | tf_op jit(solution)/shard_map/ppermute | solution.py:21
  22.2 1.9 collective-permute-start.2
  24.1 7.0 %collective-permute-start.3 = (bf16[4,512,256]{2,1,0:T(8,128)(2,1)}, bf16[4,512,256]{2,1,0:T(8,128)(2,1)}, u32[]{:S(2)}, u32[]{:S(2)}) collective-permute-start(bf16[4,512,256]{2,1,0:T(8,128)(2,1)} %param.33), channel_id=1, source_target_pairs={{1,0},{2,1},{3,2},{4,3},{5,4},{6,5},{7,6},{8,7},{9,8},{10,9},{11,1... | collective-permute-start | bytes 3145736 | tf_op jit(solution)/shard_map/ppermute | solution.py:21
  36.2 8.1 %collective-permute-done = bf16[2,1024,512]{2,1,0:T(8,128)(2,1)} collective-permute-done((bf16[2,1024,512]{2,1,0:T(8,128)(2,1)}, bf16[2,1024,512]{2,1,0:T(8,128)(2,1)}, u32[]{:S(2)}, u32[]{:S(2)}) %collective-permute-start) | collective-permute-done | bytes 2097184 | tf_op jit(solution)/shard_map/ppermute | solution.py:19
  46.2 3.0 constant_dynamic-update-slice_fusion.4
  54.2 7.0 %collective-permute-done.4 = bf16[4,256,256]{2,1,0:T(8,128)(2,1)} collective-permute-done((bf16[4,256,256]{2,1,0:T(8,128)(2,1)}, bf16[4,256,256]{2,1,0:T(8,128)(2,1)}, u32[]{:S(2)}, u32[]{:S(2)}) %collective-permute-start.4) | collective-permute-done | bytes 524320 | tf_op jit(solution)/shard_map/ppermute | solution.py:19
  62.9 2.5 pad_maximum_fusion.1
  65.4 2.0 pad_maximum_fusion
  67.5 20.9 %conditional.6 = (bf16[2,8,256,256]{2,3,1,0:T(8,128)(2,1)}) conditional(s32[]{:T(128)} %convert_element_type.100, () %tuple.66, (s32[2]{0:T(128)S(1)}, s32[2]{0:T(128)S(1)}, s32[4,8]{1,0:T(4,128)S(1)}, bf16[12,512,256]{2,1,0:T(8,128)(2,1)S(1)}, bf16[4,512,256]{2,1,0:T(8,128)(2,1)}) %tuple.67), branch_computations={%region_2.3_spmd, %region_3.6_spmd} | conditional | flops 537920512 | bytes 7607225 | solution.py:99
  67.6 20.9 %while.49 = (s32[]{:T(128)}, bf16[2,8,256,256]{2,3,1,0:T(8,128)(2,1)}, s32[2]{0:T(128)S(1)}, s32[2]{0:T(128)S(1)}, s32[4,8]{1,0:T(4,128)S(1)}, /*index=5*/bf16[1...) while((s32[]{:T(128)}, ...), condition=%wide.region_5.5_spmd, body=%wide.region_4.4_spmd.sunk | while | flops 537920512 | bytes 7607121 | solution.py:97
  72.6 2.0 gather_fusion.3
  74.7 3.3 fusion.176
  83.1 2.0 gather_fusion.3
  85.1 3.3 fusion.176
  88.4 54.3 %all-reduce.3.cloned.1.call-done = bf16[4,256,256]{2,1,0:T(8,128)(2,1)} async-done(((bf16[4,256,256]{2,1,0:T(8,128)(2,1)}), bf16[4,256,256]{2,1,0:T(8,128)(2,1)}) %all-reduce.3.cloned.1.call-update) | async-done | bytes 524304 | tf_op jit(solution)/shard_map/psum | solution.py:30
  144.4 42.6 %conditional.7 = (bf16[2,256,256]{2,1,0:T(8,128)(2,1)}, bf16[2,512,256]{2,1,0:T(8,128)(2,1)}) conditional(s32[]{:T(128)} %convert_element_type.100, () %tuple.63, (s32[2]{0:T(128)S(1)}, s32[2]{0:T(128)S(1)}, bf16[4,256,256]{2,1,0:T(8,128)(2,1)}, pred[2]{0:T(512)(128)(4,1)S(1)}, f32[4,256]{1,0:T(4,128)S(1)}, /*index=5*/s32[4,2]{0,1:T(2,128)S(1)}, ...), branch_computations={%region_12.14_spmd, %region_13.18_spmd} | conditional | flops 607127040 | bytes 12207015 | solution.py:153
  144.6 42.5 %while.52 = (s32[]{:T(128)}, bf16[2,256,256]{2,1,0:T(8,128)(2,1)}, bf16[2,512,256]{2,1,0:T(8,128)(2,1)}, s32[2]{0:T(128)S(1)}, s32[2]{0:T(128)S(1)}, /*index=5*/...) while((s32[]{:T(128)}, bf16[2,256,256]{2,1,0:T(8,128)(2,1)}, ...), condition=%wide.region_16.17_spmd, body=%wide.region_14.16_spmd.sunk | while | flops 606995968 | bytes 11420373 | solution.py:136
  149.5 2.0 gather_fusion.2
  151.6 2.4 multiply_reduce_fusion.5
  170.8 2.0 gather_fusion.2
  172.8 2.4 multiply_reduce_fusion.5
  187.9 31.6 %all-gather.3.cloned.1.call-done = bf16[8,256,256]{2,1,0:T(8,128)(2,1)} async-done(((bf16[2,256,256]{2,1,0:T(8,128)(2,1)}), bf16[8,256,256]{2,1,0:T(8,128)(2,1)}) %all-gather.3.cloned.1.call-update) | async-done | bytes 1048592 | tf_op jit(solution)/shard_map/all_gather | solution.py:160
  223.3 7.0 %collective-permute-start.7 = (bf16[4,256,256]{2,1,0:T(8,128)(2,1)S(1)}, bf16[4,256,256]{2,1,0:T(8,128)(2,1)}, u32[]{:S(2)}, u32[]{:S(2)}) collective-permute-start(bf16[4,256,256]{2,1,0:T(8,128)(2,1)S(1)} %broadcast_select_fusion.3), channel_id=1, source_target_pairs={{1,0},{2,1},{3,2},{4,3},{5,4},{6,5},{7,6},{8,7},{9,8},{10,9},{11,1... | collective-permute-start | bytes 1572872 | tf_op jit(solution)/shard_map/ppermute | solution.py:21
  230.3 30.4 %all-gather.5.cloned.1.call-done = bf16[8,512,256]{2,1,0:T(8,128)(2,1)} async-done(((bf16[2,512,256]{2,1,0:T(8,128)(2,1)}), bf16[8,512,256]{2,1,0:T(8,128)(2,1)}) %all-gather.5.cloned.1.call-update) | async-done | bytes 2097168 | tf_op jit(solution)/shard_map/all_gather | solution.py:161
  264.6 93.4 %all-reduce.5.cloned.1.call-done = bf16[4,256,256]{2,1,0:T(8,128)(2,1)} async-done(((bf16[4,256,256]{2,1,0:T(8,128)(2,1)}), bf16[4,256,256]{2,1,0:T(8,128)(2,1)}) %all-reduce.5.cloned.1.call-update) | async-done | bytes 524304 | tf_op jit(solution)/shard_map/psum | solution.py:30
  359.6 42.2 %conditional.9 = (bf16[2,256,256]{2,1,0:T(8,128)(2,1)}, bf16[2,512,256]{2,1,0:T(8,128)(2,1)}) conditional(s32[]{:T(128)} %convert_element_type.100, () %tuple.62, (s32[2]{0:T(128)S(1)}, s32[2]{0:T(128)S(1)}, bf16[4,256,256]{2,1,0:T(8,128)(2,1)S(1)}, pred[2]{0:T(512)(128)(4,1)S(1)}, f32[4,256]{1,0:T(4,128)S(1)}, /*index=5*/s32[4,2]{0,1:T(2,128)S(1)}, ...), branch_computations={%region_22.24_spmd, %region_23.28_spmd} | conditional | flops 607127040 | bytes 8012683 | solution.py:153
  360.5 41.4 %while.53 = (s32[]{:T(128)}, bf16[2,256,256]{2,1,0:T(8,128)(2,1)}, bf16[2,512,256]{2,1,0:T(8,128)(2,1)}, s32[2]{0:T(128)S(1)}, s32[2]{0:T(128)S(1)}, /*index=5*/...) while((s32[]{:T(128)}, bf16[2,256,256]{2,1,0:T(8,128)(2,1)}, ...), condition=%wide.region_26.27_spmd, body=%wide.region_24.26_spmd.sunk | while | flops 606995968 | bytes 7226041 | solution.py:136
  366.2 2.4 multiply_reduce_fusion.4
  378.6 2.6 fusion.156
  386.9 2.3 multiply_reduce_fusion.4
  399.3 2.5 fusion.156
  (134 shorter events, 61.3 us)
Async XLA Ops:
  7.2 135.6 %all-reduce.3.cloned.1.call-start = ((), (), s32[]{:S(2)}) async-start(), calls=%async_computation | async-start | bytes 1048576 | tf_op jit(solution)/shard_map/psum | solution.py:30
  7.2 37.1 %collective-permute-start = (bf16[2,1024,512]{2,1,0:T(8,128)(2,1)}, bf16[2,1024,512]{2,1,0:T(8,128)(2,1)}, u32[]{:S(2)}, u32[]{:S(2)}) collective-permute-start(bf16[2,1024,512]{2,1,0:T(8,128)(2,1)} %param.32), channel_id=1, source_target_pairs={{0,1},{1,2},{2,3},{3,4},{4,5},{5,6},{6,7},{7,8},{8,9},{9,10},{10,1... | collective-permute-start | bytes 6291464 | tf_op jit(solution)/shard_map/ppermute | solution.py:19
  9.1 41.6 %collective-permute-start.1 = (bf16[2,1024,512]{2,1,0:T(8,128)(2,1)}, bf16[2,1024,512]{2,1,0:T(8,128)(2,1)S(1)}, u32[]{:S(2)}, u32[]{:S(2)}) collective-permute-start(bf16[2,1024,512]{2,1,0:T(8,128)(2,1)} %param.32), channel_id=1, source_target_pairs={{1,0},{2,1},{3,2},{4,3},{5,4},{6,5},{7,6},{8,7},{9,8},{10,9},{11,1... | collective-permute-start | bytes 6291464 | tf_op jit(solution)/shard_map/ppermute | solution.py:21
  22.2 43.2 %collective-permute-start.2 = (bf16[4,512,256]{2,1,0:T(8,128)(2,1)}, bf16[4,512,256]{2,1,0:T(8,128)(2,1)}, u32[]{:S(2)}, u32[]{:S(2)}) collective-permute-start(bf16[4,512,256]{2,1,0:T(8,128)(2,1)} %param.33), channel_id=1, source_target_pairs={{0,1},{1,2},{2,3},{3,4},{4,5},{5,6},{6,7},{7,8},{8,9},{9,10},{10,1... | collective-permute-start | bytes 3145736 | tf_op jit(solution)/shard_map/ppermute | solution.py:19
  24.1 41.3 %collective-permute-start.3 = (bf16[4,512,256]{2,1,0:T(8,128)(2,1)}, bf16[4,512,256]{2,1,0:T(8,128)(2,1)}, u32[]{:S(2)}, u32[]{:S(2)}) collective-permute-start(bf16[4,512,256]{2,1,0:T(8,128)(2,1)} %param.33), channel_id=1, source_target_pairs={{1,0},{2,1},{3,2},{4,3},{5,4},{6,5},{7,6},{8,7},{9,8},{10,9},{11,1... | collective-permute-start | bytes 3145736 | tf_op jit(solution)/shard_map/ppermute | solution.py:21
  31.1 30.0 %collective-permute-start.4 = (bf16[4,256,256]{2,1,0:T(8,128)(2,1)}, bf16[4,256,256]{2,1,0:T(8,128)(2,1)}, u32[]{:S(2)}, u32[]{:S(2)}) collective-permute-start(bf16[4,256,256]{2,1,0:T(8,128)(2,1)} %param.34), channel_id=1, source_target_pairs={{0,1},{1,2},{2,3},{3,4},{4,5},{5,6},{6,7},{7,8},{8,9},{9,10},{10,1... | collective-permute-start | bytes 1572872 | tf_op jit(solution)/shard_map/ppermute | solution.py:19
  36.2 13.1 %copy-start.1 = (bf16[2,1024,512]{2,1,0:T(8,128)(2,1)S(1)}, bf16[2,1024,512]{2,1,0:T(8,128)(2,1)}, u32[]{:S(2)}) copy-start(bf16[2,1024,512]{2,1,0:T(8,128)(2,1)} %param.32) | copy-start | bytes 6291460
  44.3 18.6 %collective-permute-start.5 = (bf16[4,256,256]{2,1,0:T(8,128)(2,1)}, bf16[4,256,256]{2,1,0:T(8,128)(2,1)}, u32[]{:S(2)}, u32[]{:S(2)}) collective-permute-start(bf16[4,256,256]{2,1,0:T(8,128)(2,1)} %param.34), channel_id=1, source_target_pairs={{1,0},{2,1},{3,2},{4,3},{5,4},{6,5},{7,6},{8,7},{9,8},{10,9},{11,1... | collective-permute-start | bytes 1572872 | tf_op jit(solution)/shard_map/ppermute | solution.py:21
  50.8 1.6 copy-start.2
  52.4 10.5 %copy-start = (bf16[4,256,256]{2,1,0:T(8,128)(2,1)S(1)}, bf16[4,256,256]{2,1,0:T(8,128)(2,1)}, u32[]{:S(2)}) copy-start(bf16[4,256,256]{2,1,0:T(8,128)(2,1)} %param.34) | copy-start | bytes 1572868
  54.1 165.4 %all-gather.3.cloned.1.call-start = ((), (), s32[]{:S(2)}) async-start(), calls=%async_computation.1 | async-start | bytes 1310720 | tf_op jit(solution)/shard_map/all_gather | solution.py:160
  67.5 76.9 %copy-start.5 = (s32[4,2]{0,1:T(2,128)S(1)}, s32[4,2]{0,1:T(2,128)}, u32[]{:S(2)}) copy-start(s32[4,2]{0,1:T(2,128)} %param.38) | copy-start | bytes 100
  67.5 76.9 %copy-start.6 = (f32[256]{0:T(256)S(1)}, f32[256]{0:T(256)}, u32[]{:S(2)}) copy-start(f32[256]{0:T(256)} %param.36) | copy-start | bytes 3076
  67.5 76.9 %copy-start.7 = (f32[4,256]{1,0:T(4,128)S(1)}, f32[4,256]{1,0:T(4,128)}, u32[]{:S(2)}) copy-start(f32[4,256]{1,0:T(4,128)} %param.35) | copy-start | bytes 12292
  67.5 76.9 %copy-start.8 = (f32[4,8]{1,0:T(4,128)S(1)}, f32[4,8]{1,0:T(4,128)}, u32[]{:S(2)}) copy-start(f32[4,8]{1,0:T(4,128)} %param.40) | copy-start | bytes 388
  67.5 76.9 %copy-start.9 = (s32[4]{0:T(128)S(1)}, s32[4]{0:T(128)}, u32[]{:S(2)}) copy-start(s32[4]{0:T(128)} %param.37) | copy-start | bytes 52
  151.6 12.8 %copy-start.3 = (bf16[4,512,256]{2,1,0:T(8,128)(2,1)S(1)}, bf16[4,512,256]{2,1,0:T(8,128)(2,1)}, u32[]{:S(2)}) copy-start(bf16[4,512,256]{2,1,0:T(8,128)(2,1)} %get-tuple-element.1188) | copy-start | bytes 3145732 | tf_op jit(solution)/shard_map/cond/branch_1_fun/while
  172.8 12.8 %copy-start.3 = (bf16[4,512,256]{2,1,0:T(8,128)(2,1)S(1)}, bf16[4,512,256]{2,1,0:T(8,128)(2,1)}, u32[]{:S(2)}) copy-start(bf16[4,512,256]{2,1,0:T(8,128)(2,1)} %get-tuple-element.1188) | copy-start | bytes 3145732 | tf_op jit(solution)/shard_map/cond/branch_1_fun/while
  187.1 73.6 %all-gather.5.cloned.1.call-start = ((), (), s32[]{:S(2)}) async-start(), calls=%async_computation.2 | async-start | bytes 2621440 | tf_op jit(solution)/shard_map/all_gather | solution.py:161
  187.8 170.2 %all-reduce.5.cloned.1.call-start = ((), (), s32[]{:S(2)}) async-start(), calls=%async_computation.3 | async-start | bytes 1048576 | tf_op jit(solution)/shard_map/psum | solution.py:30
  221.4 41.0 %collective-permute-start.6 = (bf16[4,256,256]{2,1,0:T(8,128)(2,1)S(1)}, bf16[4,256,256]{2,1,0:T(8,128)(2,1)S(1)}, u32[]{:S(2)}, u32[]{:S(2)}) collective-permute-start(bf16[4,256,256]{2,1,0:T(8,128)(2,1)S(1)} %broadcast_select_fusion.3), channel_id=1, source_target_pairs={{0,1},{1,2},{2,3},{3,4},{4,5},{5,6},{6,7},{7,8},{8,9},{9,10},{10,1... | collective-permute-start | bytes 1572872 | tf_op jit(solution)/shard_map/ppermute | solution.py:19
  223.3 39.9 %collective-permute-start.7 = (bf16[4,256,256]{2,1,0:T(8,128)(2,1)S(1)}, bf16[4,256,256]{2,1,0:T(8,128)(2,1)}, u32[]{:S(2)}, u32[]{:S(2)}) collective-permute-start(bf16[4,256,256]{2,1,0:T(8,128)(2,1)S(1)} %broadcast_select_fusion.3), channel_id=1, source_target_pairs={{1,0},{2,1},{3,2},{4,3},{5,4},{6,5},{7,6},{8,7},{9,8},{10,9},{11,1... | collective-permute-start | bytes 1572872 | tf_op jit(solution)/shard_map/ppermute | solution.py:21
  262.4 0.8 copy-start.4
Sparse Core Ops, SparseCore 0:
  54.2 88.4 all-reduce.2
  187.2 32.1 all-gather.2
  222.1 38.5 all-gather.4
  262.9 95.0 all-reduce.4
where the time goes:
time: 410 us; the launch traced here: 408 us
  waiting for transfers between devices  227 us (55%)
  loops' own time  42 us (10%)
  local copies, waits for them, and re-layouts  40.2 us (10%)
  starting transfers between devices  36.7 us (9%)
  matrix products  24.3 us (6%)
  other arithmetic  23.8 us (6%)
  between operations  14.1 us (3%)
    psum x2, waiting for transfers between devices, from_root(): return lax.psum(kept, axis)  148 us
    another operation x2, loops' own time, refresh(): return lax.map(refresh_one_slot, slot_ids)  34.3 us
    all_gather x1, waiting for transfers between devices, local(): lax.all_gather(slot_amps, 'role', axis=0, tiled=True)  31.6 us
    all_gather x1, waiting for transfers between devices, local(): lax.all_gather(slot_orbs, 'role', axis=0, tiled=True)  30.4 us
    ppermute x4, starting transfers between devices, extended(): lax.ppermute(head, axis, [((i + 1) % count, i) for i in range(count)])  28.9 us
    ppermute x4, waiting for transfers between devices, extended(): lax.ppermute(tail, axis, [(i, (i + 1) % count) for i in range(count)])  15.1 us
    dot_general x4, matrix products, refresh_one_slot(): jnp.einsum('kbd,ked->kbe', middle, intersection, preferred_element_type=j...  9.55 us
  transfers between devices with their start and end apart: 12, of which 7 were waited for; matrix products, arithmetic and copies ran while one was open for 8% of the time, Pallas kernels for 0%

commit v1 on v0

--- a/solution.py
+++ b/solution.py
@@ -27,7 +27,7 @@
 
 def from_root(value, axis, source):
     kept = jnp.where(lax.axis_index(axis) == source, value, 0).astype(value.dtype)
-    return lax.psum(kept, axis)
+    return jnp.sum(lax.all_gather(kept, axis), axis=0)
 
 
 def local(

time: 410 us -> 339 us (0.83)
  the two profiles are of different devices: /device:TPU:16 before, /device:TPU:8 now
where the time goes in v1:
time: 339 us; the launch traced here: 337 us
  waiting for transfers between devices  152 us (45%)
  loops' own time  42.1 us (12%)
  starting transfers between devices  41.8 us (12%)
  local copies, waits for them, and re-layouts  36.3 us (11%)
  matrix products  26.5 us (8%)
  other arithmetic  24.7 us (7%)
  between operations  14.1 us (4%)
    all_gather x2, waiting for transfers between devices, from_root(): return jnp.sum(lax.all_gather(kept, axis), axis=0)  43.6 us
    all_gather x1, waiting for transfers between devices, local(): lax.all_gather(slot_orbs, 'role', axis=0, tiled=True)  37.9 us
    another operation x2, loops' own time, refresh(): return lax.map(refresh_one_slot, slot_ids)  35.4 us
    ppermute x4, starting transfers between devices, extended(): lax.ppermute(head, axis, [((i + 1) % count, i) for i in range(count)])  33.9 us
    ppermute x4, waiting for transfers between devices, extended(): lax.ppermute(tail, axis, [(i, (i + 1) % count) for i in range(count)])  33.1 us
    all_gather x1, waiting for transfers between devices, local(): lax.all_gather(slot_amps, 'role', axis=0, tiled=True)  32.7 us
    dot_general x4, matrix products, refresh_one_slot(): jnp.dot(coeff[pair_at], fresh_amp, preferred_element_type=jnp.float32)  10.3 us
    dot_general x4, matrix products, refresh_one_slot(): jnp.einsum('kbd,ked->kbe', middle, intersection, preferred_element_type=j...  9.36 us
  transfers between devices with their start and end apart: 12, of which 9 were waited for; matrix products, arithmetic and copies ran while one was open for 8% of the time, Pallas kernels for 0%

profile of v1, /device:TPU:8, one launch (start us, length us, event | category | flops | bytes accessed | tf_op | source)
XLA Modules:
  0.0 337.1 jit_solution(7923496088769236142)
XLA Ops:
  9.1 13.0 %collective-permute-start.1 = (bf16[2,1024,512]{2,1,0:T(8,128)(2,1)}, bf16[2,1024,512]{2,1,0:T(8,128)(2,1)S(1)}, u32[]{:S(2)}, u32[]{:S(2)}) collective-permute-start(bf16[2,1024,512]{2,1,0:T(8,128)(2,1)} %param.32), channel_id=1, source_target_pairs={{1,0},{2,1},{3,2},{4,3},{5,4},{6,5},{7,6},{8,7},{9,8},{10,9},{11,1... | collective-permute-start | bytes 6291464 | tf_op jit(solution)/shard_map/ppermute | solution.py:21
  22.9 21.4 %collective-permute-done = bf16[2,1024,512]{2,1,0:T(8,128)(2,1)} collective-permute-done((bf16[2,1024,512]{2,1,0:T(8,128)(2,1)}, bf16[2,1024,512]{2,1,0:T(8,128)(2,1)}, u32[]{:S(2)}, u32[]{:S(2)}) %collective-permute-start) | collective-permute-done | bytes 2097184 | tf_op jit(solution)/shard_map/ppermute | solution.py:19
  44.3 3.1 constant_dynamic-update-slice_fusion.4
  54.1 7.0 %collective-permute-start.3 = (bf16[4,512,256]{2,1,0:T(8,128)(2,1)S(1)}, bf16[4,512,256]{2,1,0:T(8,128)(2,1)}, u32[]{:S(2)}, u32[]{:S(2)}) collective-permute-start(bf16[4,512,256]{2,1,0:T(8,128)(2,1)S(1)} %copy-done.3), channel_id=1, source_target_pairs={{1,0},{2,1},{3,2},{4,3},{5,4},{6,5},{7,6},{8,7},{9,8},{10,9},{11,1... | collective-permute-start | bytes 3145736 | tf_op jit(solution)/shard_map/ppermute | solution.py:21
  63.0 7.0 %collective-permute-start.5 = (bf16[4,256,256]{2,1,0:T(8,128)(2,1)S(1)}, bf16[4,256,256]{2,1,0:T(8,128)(2,1)}, u32[]{:S(2)}, u32[]{:S(2)}) collective-permute-start(bf16[4,256,256]{2,1,0:T(8,128)(2,1)S(1)} %copy-done.1), channel_id=1, source_target_pairs={{1,0},{2,1},{3,2},{4,3},{5,4},{6,5},{7,6},{8,7},{9,8},{10,9},{11,1... | collective-permute-start | bytes 1572872 | tf_op jit(solution)/shard_map/ppermute | solution.py:21
  70.4 6.8 %collective-permute-done.4 = bf16[4,256,256]{2,1,0:T(8,128)(2,1)S(1)} collective-permute-done((bf16[4,256,256]{2,1,0:T(8,128)(2,1)S(1)}, bf16[4,256,256]{2,1,0:T(8,128)(2,1)S(1)}, u32[]{:S(2)}, u32[]{:S(2)}) %collective-permute-start.4) | collective-permute-done | bytes 524320 | tf_op jit(solution)/shard_map/ppermute | solution.py:19
  79.0 2.4 pad_maximum_fusion.1
  82.3 2.0 pad_maximum_fusion
  84.4 19.9 %conditional.6 = (bf16[2,8,256,256]{2,3,1,0:T(8,128)(2,1)}) conditional(s32[]{:T(128)} %convert_element_type.104, () %tuple.66, (s32[2]{0:T(128)S(1)}, s32[2]{0:T(128)S(1)}, s32[4,8]{1,0:T(4,128)S(1)}, bf16[12,512,256]{2,1,0:T(8,128)(2,1)S(1)}, bf16[4,512,256]{2,1,0:T(8,128)(2,1)}) %tuple.67), branch_computations={%region_2.3_spmd, %region_3.6_spmd} | conditional | flops 537920512 | bytes 7607225 | solution.py:99
  84.4 19.9 %while.49 = (s32[]{:T(128)}, bf16[2,8,256,256]{2,3,1,0:T(8,128)(2,1)}, s32[2]{0:T(128)S(1)}, s32[2]{0:T(128)S(1)}, s32[4,8]{1,0:T(4,128)S(1)}, /*index=5*/bf16[1...) while((s32[]{:T(128)}, ...), condition=%wide.region_5.5_spmd, body=%wide.region_4.4_spmd.sunk | while | flops 537920512 | bytes 7607121 | solution.py:97
  88.9 2.1 gather_fusion.3
  91.0 3.3 fusion.176
  98.7 2.1 gather_fusion.3
  100.8 3.5 %fusion.176 = bf16[2,8,256,256]{2,3,1,0:T(8,128)(2,1)} fusion(bf16[2,8,256,256]{2,3,1,0:T(8,128)(2,1)} %get-tuple-element.1206, s32[]{:T(128)} %get-tuple-element.1205, bf16[8,512,256]{2,1,0:T(8,128)(2,1)} %gather_fusion.3, bf16[4,512,256]{2,1,0:T(8,128)(2,1)} %get-tuple-element.1222, s32[]{:T(128)S(6)} %select_n.217), kind=kOutput, calls=%fused_computation.51.clone.1 | convolution fusion | flops 537919488 | bytes 3408388 | tf_op jit(solution)/shard_map/cond/branch_1_fun/while/body/eval_jaxpr/mb,kmc->kbc/dot_general | solution.py:91
  104.4 16.1 %all-gather.11.cloned.1.call-done = bf16[16,256,256]{2,1,0:T(8,128)(2,1)} async-done(((bf16[4,256,256]{2,1,0:T(8,128)(2,1)}), bf16[16,256,256]{2,1,0:T(8,128)(2,1)}) %all-gather.11.cloned.1.call-update) | async-done | bytes 2097168 | tf_op jit(solution)/shard_map/all_gather | solution.py:30
  123.1 42.9 %conditional.7 = (bf16[2,256,256]{2,1,0:T(8,128)(2,1)}, bf16[2,512,256]{2,1,0:T(8,128)(2,1)}) conditional(s32[]{:T(128)} %convert_element_type.104, () %tuple.63, (s32[2]{0:T(128)S(1)}, s32[2]{0:T(128)S(1)}, bf16[4,256,256]{2,1,0:T(8,128)(2,1)}, pred[2]{0:T(512)(128)(4,1)S(1)}, f32[4,256]{1,0:T(4,128)S(1)}, /*index=5*/s32[4,2]{0,1:T(2,128)S(1)}, ...), branch_computations={%region_12.14_spmd, %region_13.18_spmd} | conditional | flops 607127040 | bytes 8012683 | solution.py:153
  123.2 42.8 %while.52 = (s32[]{:T(128)}, bf16[2,256,256]{2,1,0:T(8,128)(2,1)}, bf16[2,512,256]{2,1,0:T(8,128)(2,1)}, s32[2]{0:T(128)S(1)}, s32[2]{0:T(128)S(1)}, /*index=5*/...) while((s32[]{:T(128)}, bf16[2,256,256]{2,1,0:T(8,128)(2,1)}, ...), condition=%wide.region_16.17_spmd, body=%wide.region_14.16_spmd.sunk | while | flops 606995968 | bytes 7226041 | solution.py:136
  128.9 2.3 multiply_reduce_fusion.5
  142.0 2.6 fusion.172
  150.3 2.4 multiply_reduce_fusion.5
  163.4 2.6 fusion.172
  166.8 37.9 %all-gather.9.cloned.1.call-done = bf16[8,512,256]{2,1,0:T(8,128)(2,1)} async-done(((bf16[2,512,256]{2,1,0:T(8,128)(2,1)}), bf16[8,512,256]{2,1,0:T(8,128)(2,1)}) %all-gather.9.cloned.1.call-update) | async-done | bytes 2097168 | tf_op jit(solution)/shard_map/all_gather | solution.py:161
  206.4 32.7 %all-gather.7.cloned.1.call-done = bf16[8,256,256]{2,1,0:T(8,128)(2,1)} async-done(((bf16[2,256,256]{2,1,0:T(8,128)(2,1)}), bf16[8,256,256]{2,1,0:T(8,128)(2,1)}) %all-gather.7.cloned.1.call-update) | async-done | bytes 1048592 | tf_op jit(solution)/shard_map/all_gather | solution.py:160
  243.0 7.0 %collective-permute-start.7 = (bf16[4,256,256]{2,1,0:T(8,128)(2,1)S(1)}, bf16[4,256,256]{2,1,0:T(8,128)(2,1)S(1)}, u32[]{:S(2)}, u32[]{:S(2)}) collective-permute-start(bf16[4,256,256]{2,1,0:T(8,128)(2,1)S(1)} %broadcast_select_fusion.3), channel_id=1, source_target_pairs={{1,0},{2,1},{3,2},{4,3},{5,4},{6,5},{7,6},{8,7},{9,8},{10,9},{11,1... | collective-permute-start | bytes 1572872 | tf_op jit(solution)/shard_map/ppermute | solution.py:21
  250.0 4.9 %collective-permute-done.6 = bf16[4,256,256]{2,1,0:T(8,128)(2,1)S(1)} collective-permute-done((bf16[4,256,256]{2,1,0:T(8,128)(2,1)S(1)}, bf16[4,256,256]{2,1,0:T(8,128)(2,1)S(1)}, u32[]{:S(2)}, u32[]{:S(2)}) %collective-permute-start.6) | collective-permute-done | bytes 524320 | tf_op jit(solution)/shard_map/ppermute | solution.py:19
  256.8 27.6 %all-gather.13.cloned.1.call-done = bf16[16,256,256]{2,1,0:T(8,128)(2,1)} async-done(((bf16[4,256,256]{2,1,0:T(8,128)(2,1)}), bf16[16,256,256]{2,1,0:T(8,128)(2,1)}) %all-gather.13.cloned.1.call-update) | async-done | bytes 2097168 | tf_op jit(solution)/shard_map/all_gather | solution.py:30
  286.9 43.6 %conditional.9 = (bf16[2,256,256]{2,1,0:T(8,128)(2,1)}, bf16[2,512,256]{2,1,0:T(8,128)(2,1)}) conditional(s32[]{:T(128)} %convert_element_type.104, () %tuple.62, (s32[2]{0:T(128)S(1)}, s32[2]{0:T(128)S(1)}, bf16[4,256,256]{2,1,0:T(8,128)(2,1)S(1)}, pred[2]{0:T(512)(128)(4,1)S(1)}, f32[4,256]{1,0:T(4,128)S(1)}, /*index=5*/s32[4,2]{0,1:T(2,128)S(1)}, ...), branch_computations={%region_22.24_spmd, %region_23.28_spmd} | conditional | flops 607127040 | bytes 8012683 | solution.py:153
  287.8 42.8 %while.53 = (s32[]{:T(128)}, bf16[2,256,256]{2,1,0:T(8,128)(2,1)}, bf16[2,512,256]{2,1,0:T(8,128)(2,1)}, s32[2]{0:T(128)S(1)}, s32[2]{0:T(128)S(1)}, /*index=5*/...) while((s32[]{:T(128)}, bf16[2,256,256]{2,1,0:T(8,128)(2,1)}, ...), condition=%wide.region_26.27_spmd, body=%wide.region_24.26_spmd.sunk | while | flops 606995968 | bytes 7226041 | solution.py:136
  293.5 2.3 multiply_reduce_fusion.4
  306.5 2.6 fusion.156
  314.8 2.4 multiply_reduce_fusion.4
  328.0 2.6 fusion.156
  (138 shorter events, 63.1 us)
Async XLA Ops:
  7.2 113.3 %all-gather.11.cloned.1.call-start = ((), (), s32[]{:S(2)}) async-start(), calls=%async_computation.2 | async-start | bytes 2621440 | tf_op jit(solution)/shard_map/all_gather | solution.py:30
  7.2 37.1 %collective-permute-start = (bf16[2,1024,512]{2,1,0:T(8,128)(2,1)}, bf16[2,1024,512]{2,1,0:T(8,128)(2,1)}, u32[]{:S(2)}, u32[]{:S(2)}) collective-permute-start(bf16[2,1024,512]{2,1,0:T(8,128)(2,1)} %param.32), channel_id=1, source_target_pairs={{0,1},{1,2},{2,3},{3,4},{4,5},{5,6},{6,7},{7,8},{8,9},{9,10},{10,1... | collective-permute-start | bytes 6291464 | tf_op jit(solution)/shard_map/ppermute | solution.py:19
  9.1 39.7 %collective-permute-start.1 = (bf16[2,1024,512]{2,1,0:T(8,128)(2,1)}, bf16[2,1024,512]{2,1,0:T(8,128)(2,1)S(1)}, u32[]{:S(2)}, u32[]{:S(2)}) collective-permute-start(bf16[2,1024,512]{2,1,0:T(8,128)(2,1)} %param.32), channel_id=1, source_target_pairs={{1,0},{2,1},{3,2},{4,3},{5,4},{6,5},{7,6},{8,7},{9,8},{10,9},{11,1... | collective-permute-start | bytes 6291464 | tf_op jit(solution)/shard_map/ppermute | solution.py:21
  22.9 24.5 %copy-start.2 = (bf16[2,1024,512]{2,1,0:T(8,128)(2,1)S(1)}, bf16[2,1024,512]{2,1,0:T(8,128)(2,1)}, u32[]{:S(2)}) copy-start(bf16[2,1024,512]{2,1,0:T(8,128)(2,1)} %param.32) | copy-start | bytes 6291460
  48.8 1.6 copy-start.3
  50.4 10.6 %copy-start.1 = (bf16[4,256,256]{2,1,0:T(8,128)(2,1)S(1)}, bf16[4,256,256]{2,1,0:T(8,128)(2,1)}, u32[]{:S(2)}) copy-start(bf16[4,256,256]{2,1,0:T(8,128)(2,1)} %param.34) | copy-start | bytes 1572868
  50.4 19.6 %copy-start.9 = (s32[4]{0:T(128)S(1)}, s32[4]{0:T(128)}, u32[]{:S(2)}) copy-start(s32[4]{0:T(128)} %param.41) | copy-start | bytes 52
  50.4 20.0 %copy-start.8 = (s32[4,8]{1,0:T(4,128)S(1)}, s32[4,8]{1,0:T(4,128)}, u32[]{:S(2)}) copy-start(s32[4,8]{1,0:T(4,128)} %param.39) | copy-start | bytes 388
  52.1 152.6 %all-gather.9.cloned.1.call-start = ((), (), s32[]{:S(2)}) async-start(), calls=%async_computation.1 | async-start | bytes 2621440 | tf_op jit(solution)/shard_map/all_gather | solution.py:161
  52.2 29.2 %collective-permute-start.2 = (bf16[4,512,256]{2,1,0:T(8,128)(2,1)S(1)}, bf16[4,512,256]{2,1,0:T(8,128)(2,1)S(1)}, u32[]{:S(2)}, u32[]{:S(2)}) collective-permute-start(bf16[4,512,256]{2,1,0:T(8,128)(2,1)S(1)} %copy-done.3), channel_id=1, source_target_pairs={{0,1},{1,2},{2,3},{3,4},{4,5},{5,6},{6,7},{7,8},{8,9},{9,10},{10,1... | collective-permute-start | bytes 3145736 | tf_op jit(solution)/shard_map/ppermute | solution.py:19
  54.1 28.2 %collective-permute-start.3 = (bf16[4,512,256]{2,1,0:T(8,128)(2,1)S(1)}, bf16[4,512,256]{2,1,0:T(8,128)(2,1)}, u32[]{:S(2)}, u32[]{:S(2)}) collective-permute-start(bf16[4,512,256]{2,1,0:T(8,128)(2,1)S(1)} %copy-done.3), channel_id=1, source_target_pairs={{1,0},{2,1},{3,2},{4,3},{5,4},{6,5},{7,6},{8,7},{9,8},{10,9},{11,1... | collective-permute-start | bytes 3145736 | tf_op jit(solution)/shard_map/ppermute | solution.py:21
  61.1 16.1 %collective-permute-start.4 = (bf16[4,256,256]{2,1,0:T(8,128)(2,1)S(1)}, bf16[4,256,256]{2,1,0:T(8,128)(2,1)S(1)}, u32[]{:S(2)}, u32[]{:S(2)}) collective-permute-start(bf16[4,256,256]{2,1,0:T(8,128)(2,1)S(1)} %copy-done.1), channel_id=1, source_target_pairs={{0,1},{1,2},{2,3},{3,4},{4,5},{5,6},{6,7},{7,8},{8,9},{9,10},{10,1... | collective-permute-start | bytes 1572872 | tf_op jit(solution)/shard_map/ppermute | solution.py:19
  63.0 16.0 %collective-permute-start.5 = (bf16[4,256,256]{2,1,0:T(8,128)(2,1)S(1)}, bf16[4,256,256]{2,1,0:T(8,128)(2,1)}, u32[]{:S(2)}, u32[]{:S(2)}) collective-permute-start(bf16[4,256,256]{2,1,0:T(8,128)(2,1)S(1)} %copy-done.1), channel_id=1, source_target_pairs={{1,0},{2,1},{3,2},{4,3},{5,4},{6,5},{7,6},{8,7},{9,8},{10,9},{11,1... | collective-permute-start | bytes 1572872 | tf_op jit(solution)/shard_map/ppermute | solution.py:21
  81.3 1.0 copy-start.4
  104.3 18.7 %copy-start = (bf16[12,256,256]{2,1,0:T(8,128)(2,1)S(1)}, bf16[12,256,256]{2,1,0:T(8,128)(2,1)}, u32[]{:S(2)}) copy-start(bf16[12,256,256]{2,1,0:T(8,128)(2,1)} %pad_maximum_fusion.1) | copy-start | bytes 4718596
  104.3 18.7 %copy-start.5 = (s32[4,2]{0,1:T(2,128)S(1)}, s32[4,2]{0,1:T(2,128)}, u32[]{:S(2)}) copy-start(s32[4,2]{0,1:T(2,128)} %param.38) | copy-start | bytes 100
  104.3 18.7 %copy-start.6 = (f32[256]{0:T(256)S(1)}, f32[256]{0:T(256)}, u32[]{:S(2)}) copy-start(f32[256]{0:T(256)} %param.36) | copy-start | bytes 3076
  104.3 18.7 %copy-start.7 = (f32[4,256]{1,0:T(4,128)S(1)}, f32[4,256]{1,0:T(4,128)}, u32[]{:S(2)}) copy-start(f32[4,256]{1,0:T(4,128)} %param.35) | copy-start | bytes 12292
  104.3 18.7 %copy-start.10 = (f32[4,8]{1,0:T(4,128)S(1)}, f32[4,8]{1,0:T(4,128)}, u32[]{:S(2)}) copy-start(f32[4,8]{1,0:T(4,128)} %param.40) | copy-start | bytes 388
  104.3 18.7 %copy-start.11 = (s32[4]{0:T(128)S(1)}, s32[4]{0:T(128)}, u32[]{:S(2)}) copy-start(s32[4]{0:T(128)} %param.37) | copy-start | bytes 52
  166.0 73.1 %all-gather.7.cloned.1.call-start = ((), (), s32[]{:S(2)}) async-start(), calls=%async_computation | async-start | bytes 1310720 | tf_op jit(solution)/shard_map/all_gather | solution.py:160
  166.8 117.6 %all-gather.13.cloned.1.call-start = ((), (), s32[]{:S(2)}) async-start(), calls=%async_computation.3 | async-start | bytes 2621440 | tf_op jit(solution)/shard_map/all_gather | solution.py:30
  241.1 13.8 %collective-permute-start.6 = (bf16[4,256,256]{2,1,0:T(8,128)(2,1)S(1)}, bf16[4,256,256]{2,1,0:T(8,128)(2,1)S(1)}, u32[]{:S(2)}, u32[]{:S(2)}) collective-permute-start(bf16[4,256,256]{2,1,0:T(8,128)(2,1)S(1)} %broadcast_select_fusion.3), channel_id=1, source_target_pairs={{0,1},{1,2},{2,3},{3,4},{4,5},{5,6},{6,7},{7,8},{8,9},{9,10},{10,1... | collective-permute-start | bytes 1572872 | tf_op jit(solution)/shard_map/ppermute | solution.py:19
  243.0 13.6 %collective-permute-start.7 = (bf16[4,256,256]{2,1,0:T(8,128)(2,1)S(1)}, bf16[4,256,256]{2,1,0:T(8,128)(2,1)S(1)}, u32[]{:S(2)}, u32[]{:S(2)}) collective-permute-start(bf16[4,256,256]{2,1,0:T(8,128)(2,1)S(1)} %broadcast_select_fusion.3), channel_id=1, source_target_pairs={{1,0},{2,1},{3,2},{4,3},{5,4},{6,5},{7,6},{8,7},{9,8},{10,9},{11,1... | collective-permute-start | bytes 1572872 | tf_op jit(solution)/shard_map/ppermute | solution.py:21
Sparse Core Ops, SparseCore 0:
  52.2 68.1 all-gather.10
  166.2 38.5 all-gather.8
  207.4 31.6 all-gather.6
  241.7 42.6 all-gather.12
